TPU v7x, 32 devices: a whole 2x2x4 slice. The times are simulated.
32 devices in a mesh: band: 2 (over y), dom: 16 (over z, x, core).
Axes of the slice: x: 2, y: 2, z: 4, core: 2. Of those that a mesh axis runs over, the one named last changes fastest.
Arguments:
- states_in: float32 [128, 16384], P('band', 'dom'), may hold values from -6 to 6
- stiffness: float32 [343, 343], replicated, may hold values from -2 to 2, as said below
- cell_scale: float32 [96], P('dom'), may hold values from 0.5 to 2
- potential: float32 [16384], P('dom'), may hold values from 0 to 2
- inv_mass_sqrt: float32 [16384], P('dom'), may hold values from 0.25 to 1.75
- cell_nodes: int32 [96, 343], P('dom'), may hold values from 0 to 1151, as said below
- shared_nodes: int32 [2048], P('dom'), may hold values from 0 to 1023, as said below
Outputs:
- filtered: float32 [128, 16384], P('band', 'dom')
- margin: float32 [128, 128], P('band')
Inputs may be any that keep to these rules, and one draw needn't show every extreme that they name: `stiffness`: symmetric. `cell_nodes`: in the cells of a subdomain, an entry below 1024 is one of its own nodes and an entry l of 1024 or more stands for entry l - 1024 of the next subdomain's (cyclically) shared_nodes list; every value from 0 to 1151 occurs in the subdomain's cells. `shared_nodes`: the 128 entries of each subdomain are distinct.
All inputs are finite; a program needn't handle non-finite values.
Results may differ from a plain program's by a relative error of at most 0.0001.
Values sent between devices are 32-bit elements; how exact they have to be, the bound alone decides.
A program may use at most 64 MiB of HBM per device.

v0:
```python
import functools

import jax
import jax.numpy as jnp
from jax import lax
from jax.experimental import pallas as pl
from jax.experimental.pallas import tpu as pltpu
from jax.sharding import PartitionSpec as P

DEGREE = 3
CENTER = 1.0
HALF_WIDTH = 4.0
LANES = 128
F32, BF16 = jnp.float32, jnp.bfloat16


def stacked_parts(value):
    high = value.astype(BF16)
    low = (value - high.astype(F32)).astype(BF16)
    return jnp.concatenate([high, low], axis=0)


def folded(value):
    half = value.shape[0] // 2
    return value[:half] + value[half:]


def dot(a, b):
    return jnp.dot(a, b, preferred_element_type=F32)


def dot_nt(a, b):
    return lax.dot_general(a, b, (((1,), (1,)), ((), ())), preferred_element_type=F32)


def one_hot(a, b):
    return jnp.where(a == b, 1.0, 0.0).astype(F32)


def kernel(
    n_band, n_dom, inner,
    x_hbm, stiff_hbm, scale_hbm, pot_hbm, mass_hbm, cells_hbm, shared_hbm,
    filt_ref, margin_ref,
    x_ref, stiff_ref, scale_ref, pot_ref, mass_ref, cells_ref, shared_ref, load_sem,
    idx, stiff_pad, stiff_hi, stiff_lo, gather, scatter, spread, lead,
    lead_send, lead_recv, ret_send, ret_recv, last_recv, part_send, part_recv,
    uu, yy, zz, block_send, blocks, gram, gram_recv, chunk, chunk_recv, final,
    lead_sem, ret_sem, last_sem, part_sem, block_sem, gram_sem, chunk_sem, final_sem,
):
    rows, owned = x_ref.shape
    cells, npc = cells_ref.shape
    shared = shared_ref.shape[1]
    width = idx.shape[1]
    edge = 2 * shared
    outer = n_dom // inner
    band, dom = lax.axis_index("band"), lax.axis_index("dom")
    after, before = lax.rem(dom + 1, n_dom), lax.rem(dom + n_dom - 1, n_dom)
    place, line = lax.rem(dom, inner), dom // inner

    def turned(value, by, size):
        return lax.rem(value + by, size)

    def at(b, d):
        return {"band": b, "dom": d}

    pairs = (
        (shared_hbm, shared_ref), (mass_hbm, mass_ref), (pot_hbm, pot_ref), (x_hbm, x_ref),
        (cells_hbm, cells_ref), (stiff_hbm, stiff_ref), (scale_hbm, scale_ref))
    loads = [pltpu.make_async_copy(src, dst, load_sem.at[k]) for k, (src, dst) in enumerate(pairs)]
    first_loads, later_loads = loads[:4], loads[4:]
    barrier = pltpu.get_barrier_semaphore()
    greeted = 0
    for k in range(n_band):
        other = turned(band, k, n_band)
        opposite = turned(band, n_band - k, n_band)
        pl.semaphore_signal(barrier, inc=1, device_id=at(other, after))
        pl.semaphore_signal(barrier, inc=1, device_id=at(opposite, before))
        greeted += 2
        if k:
            pl.semaphore_signal(barrier, inc=1, device_id=at(other, dom))
            greeted += 1
    for k in range(1, inner):
        pl.semaphore_signal(
            barrier, inc=1, device_id=at(band, line * inner + turned(place, k, inner)))
        greeted += 1
    for k in range(1, outer):
        pl.semaphore_signal(
            barrier, inc=1, device_id=at(band, turned(line, k, outer) * inner + place))
        greeted += 1

    for load in loads:
        load.start()
    started = []

    def send(src, dst, sems, slot, device):
        copy = pltpu.make_async_remote_copy(
            src_ref=src, dst_ref=dst, send_sem=sems.at[0, slot], recv_sem=sems.at[1, slot],
            device_id=device, device_id_type=pl.DeviceIdType.MESH)
        copy.start()
        started.append(copy)
        return copy

    for load in first_loads:
        load.wait()
    mass, pot = mass_ref[...], pot_ref[...]
    shared_row = shared_ref[...]
    lead[0:rows, :] = x_ref[...]
    lead[rows:rows + 8, :] = jnp.concatenate(
        [mass, pot, jnp.zeros((6, owned), F32)], axis=0)
    pick = one_hot(lax.broadcasted_iota(jnp.int32, (owned, shared), 0), shared_row)
    lead_send[...] = jnp.dot(
        lead[...], pick, precision=lax.Precision.HIGHEST, preferred_element_type=F32)
    pl.semaphore_wait(barrier, greeted)
    lead_copy = send(lead_send, lead_recv, lead_sem, 0, at(band, before))

    for load in later_loads:
        load.wait()
    idx[...] = jnp.full(idx.shape, -1.0, F32)
    idx[0:cells, 0:npc] = cells_ref[...].astype(F32)
    stiff_pad[...] = jnp.zeros(stiff_pad.shape, F32)
    stiff_pad[0:npc, 0:npc] = stiff_ref[...]
    high = stiff_pad[...].astype(BF16)
    stiff_hi[...] = high
    stiff_lo[...] = (stiff_pad[...] - high.astype(F32)).astype(BF16)
    shared_f = shared_row.astype(F32)
    shared_col = jnp.broadcast_to(shared_f, (LANES, shared)).T
    for k in range(owned // LANES):
        lane = lax.broadcasted_iota(jnp.int32, (shared, LANES), 1) + k * LANES
        spread[:, k * LANES:(k + 1) * LANES] = one_hot(shared_col, lane.astype(F32)).astype(BF16)
    local = owned + shared
    node = lax.broadcasted_iota(jnp.int32, (LANES, width), 0).astype(F32)
    lane = lax.broadcasted_iota(jnp.int32, (width, LANES), 1).astype(F32)
    shared_wide = jnp.concatenate([shared_col] * (width // LANES), axis=1)
    for c in range(cells):
        slot_row = jnp.broadcast_to(idx[c:c + 1, :], (LANES, width))
        slot_col = slot_row.T
        span = slice(c * width, (c + 1) * width)
        for k in range(local // LANES):
            tile = slice(k * LANES, (k + 1) * LANES)
            gather[c, tile, :] = one_hot(node + float(k * LANES), slot_row).astype(BF16)
            scatter[span, tile] = one_hot(lane + float(k * LANES), slot_col).astype(BF16)
        gather[c, local:, :] = one_hot(shared_wide, slot_row).astype(BF16)
        scatter[span, local:] = one_hot(shared_f, slot_col).astype(BF16)

    mass_shared, pot_shared = lead_send[rows:rows + 1, :], lead_send[rows + 1:rows + 2, :]
    partial = x_ref[...]
    current_shared = lead_send[0:rows, :]
    previous, previous_shared = None, None
    returned = None
    for t in range(DEGREE):
        last = t == DEGREE - 1
        factor = (1.0 if t == 0 else 2.0) / HALF_WIDTH
        uu[...] = stacked_parts(mass * partial)
        for c in range(cells):
            yy[c] = dot(uu[...], gather[c, 0:owned, :])
        if t == 0:
            lead_copy.wait_recv()
            mass_ghost = lead_recv[rows:rows + 1, :]
            ghost = lead_recv[0:rows, :]
            fix = None
            outside = stacked_parts(
                jnp.concatenate([mass_ghost * ghost, jnp.zeros_like(ghost)], axis=1))
        else:
            ret_copy.wait_recv()
            part_copy.wait_recv()
            fix = earlier * mass_shared * ret_recv[t - 1]
            ghost = part_recv[t - 1] + earlier * mass_ghost * returned
            current_shared = part + fix
            outside = stacked_parts(
                jnp.concatenate([mass_ghost * ghost, mass_shared * fix], axis=1))
        for c in range(cells):
            y = stacked_parts(folded(yy[c] + dot(outside, gather[c, owned:, :])))
            z = folded(dot(y, stiff_hi[...])) + dot(y[0:rows], stiff_lo[...])
            zz[:, c * width:(c + 1) * width] = stacked_parts(z * scale_ref[c])
        border = folded(dot(zz[...], scatter[:, owned:]))
        returned = border[:, 0:shared]
        ret_send[t] = returned
        if last:
            last_copies = [
                send(ret_send.at[t], last_recv.at[band], last_sem, k,
                     at(turned(band, k, n_band), after))
                for k in range(n_band)]
        else:
            ret_copy = send(ret_send.at[t], ret_recv.at[t], ret_sem, t, at(band, after))
            part = factor * (
                mass_shared * border[:, shared:] + (pot_shared - CENTER) * current_shared)
            if t:
                part = part - previous_shared
            part_send[t] = part
            part_copy = send(part_send.at[t], part_recv.at[t], part_sem, t, at(band, before))
        current = partial
        if t:
            current = current + folded(dot(stacked_parts(fix), spread[...]))
        sums = folded(dot(zz[...], scatter[:, 0:owned]))
        partial = factor * (mass * sums + (pot - CENTER) * current)
        if t:
            partial = partial - previous
        previous, previous_shared = current, current_shared
        earlier = factor

    block_send[...] = partial
    blocks[band] = partial
    block_copies = [
        send(block_send, blocks.at[band], block_sem, k - 1, at(turned(band, k, n_band), dom))
        for k in range(1, n_band)]
    for copy in last_copies:
        copy.wait_recv()
    for copy in block_copies:
        copy.wait_recv()
    for b in range(n_band):
        fix = stacked_parts(earlier * mass_shared * last_recv[b])
        blocks[b] = blocks[b] + folded(dot(fix, spread[...]))
    filtered = blocks[band]
    filt_ref[...] = filtered
    mine = stacked_parts(filtered)
    depth = rows // inner
    pieces = []
    for b in range(n_band):
        theirs = stacked_parts(blocks[b])
        pieces.append(folded(dot_nt(mine, theirs[0:rows])) + dot_nt(mine[0:rows], theirs[rows:]))
    product = jnp.concatenate(pieces, axis=1) * (1.0 / (owned * n_dom))
    for k in range(inner):
        gram[k] = product[k * depth:(k + 1) * depth]
    copies = []
    for k in range(1, inner):
        to = turned(place, k, inner)
        copies.append(send(
            gram.at[to], gram_recv.at[place], gram_sem, k - 1, at(band, line * inner + to)))
    gram_recv[place] = gram[place]
    for copy in copies:
        copy.wait_recv()
    total = gram_recv[0]
    for k in range(1, inner):
        total = total + gram_recv[k]
    chunk[...] = total
    copies = [
        send(chunk, chunk_recv.at[line], chunk_sem, k - 1,
             at(band, turned(line, k, outer) * inner + place))
        for k in range(1, outer)]
    chunk_recv[line] = total
    for copy in copies:
        copy.wait_recv()
    total = chunk_recv[0]
    for k in range(1, outer):
        total = total + chunk_recv[k]
    gram_out = final.at[place]
    gram_out[...] = total
    copies = [
        send(final.at[place], final.at[place], final_sem, k - 1,
             at(band, line * inner + turned(place, k, inner)))
        for k in range(1, inner)]
    for copy in copies:
        copy.wait_recv()
    for k in range(inner):
        margin_ref[k * depth:(k + 1) * depth, :] = final[k]
    for copy in started:
        copy.wait_send()


def rounded_up(value):
    return -(-value // LANES) * LANES


def per_device(
    n_band, n_dom,
    states_in, stiffness, cell_scale, potential, inv_mass_sqrt, cell_nodes, shared_nodes
):
    rows, owned = states_in.shape
    cells, npc = cell_nodes.shape
    shared = shared_nodes.shape[0]
    width = rounded_up(npc)
    nodes = owned + 2 * shared
    states = n_band * rows
    inner = 1
    while inner * inner * 4 <= n_dom:
        inner *= 2
    outer = n_dom // inner
    depth = rows // inner
    pairs = lambda count: pltpu.SemaphoreType.DMA((2, count))
    vmem = pltpu.VMEM
    in_vmem = pl.BlockSpec(memory_space=pltpu.VMEM)
    return pl.pallas_call(
        functools.partial(kernel, n_band, n_dom, inner),
        out_shape=(
            jax.ShapeDtypeStruct((rows, owned), F32),
            jax.ShapeDtypeStruct((rows, states), F32),
        ),
        in_specs=[pl.BlockSpec(memory_space=pltpu.HBM)] * 7,
        out_specs=(in_vmem, in_vmem),
        scratch_shapes=[
            vmem((rows, owned), F32),
            vmem((npc, npc), F32),
            pltpu.SMEM((cells,), F32),
            vmem((1, owned), F32),
            vmem((1, owned), F32),
            vmem((cells, npc), jnp.int32),
            vmem((1, shared), jnp.int32),
            pltpu.SemaphoreType.DMA((7,)),
            vmem((-(-cells // 8) * 8, width), F32),
            vmem((width, width), F32),
            vmem((width, width), BF16),
            vmem((width, width), BF16),
            vmem((cells, nodes, width), BF16),
            vmem((cells * width, nodes), BF16),
            vmem((shared, owned), BF16),
            vmem((rows + 8, owned), F32),
            vmem((rows + 8, shared), F32),
            vmem((rows + 8, shared), F32),
            vmem((DEGREE, rows, shared), F32),
            vmem((DEGREE - 1, rows, shared), F32),
            vmem((n_band, rows, shared), F32),
            vmem((DEGREE - 1, rows, shared), F32),
            vmem((DEGREE - 1, rows, shared), F32),
            vmem((2 * rows, owned), BF16),
            vmem((cells, 2 * rows, width), F32),
            vmem((2 * rows, cells * width), BF16),
            vmem((rows, owned), F32),
            vmem((n_band, rows, owned), F32),
            vmem((inner, depth, states), F32),
            vmem((inner, depth, states), F32),
            vmem((depth, states), F32),
            vmem((outer, depth, states), F32),
            vmem((inner, depth, states), F32),
            pairs(1),
            pairs(DEGREE - 1),
            pairs(n_band),
            pairs(DEGREE - 1),
            pairs(max(n_band - 1, 1)),
            pairs(max(inner - 1, 1)),
            pairs(max(outer - 1, 1)),
            pairs(max(inner - 1, 1)),
        ],
        compiler_params=pltpu.CompilerParams(collective_id=0, has_side_effects=True, vmem_limit_bytes=28 << 20),
    )(*[pltpu.with_memory_space_constraint(value, pltpu.HBM) for value in (
        states_in, stiffness, cell_scale, potential[None, :], inv_mass_sqrt[None, :],
        cell_nodes, shared_nodes[None, :],
    )])


def solution(mesh):
    n_band, n_dom = mesh.shape["band"], mesh.shape["dom"]
    return jax.shard_map(
        functools.partial(per_device, n_band, n_dom),
        mesh=mesh,
        in_specs=(P("band", "dom"), P(), P("dom"), P("dom"), P("dom"), P("dom", None), P("dom")),
        out_specs=(P("band", "dom"), P("band", None)),
        check_vma=False,
    )
```

profile of v0, /device:TPU:0, one launch (start us, length us, event | category | flops | bytes accessed | tf_op | source)
XLA Modules:
  0.0 41.4 jit_solution(4635585257971242709)
XLA Ops:
  0.6 39.4 %shard_map.86 = (f32[64,1024]{1,0:T(8,128)S(1)}, f32[64,128]{1,0:T(8,128)S(1)}) custom-call(f32[64,1024]{1,0:T(8,128)} %x_hbm.1, f32[343,343]{1,0:T(8,128)} %stiff_hbm.1, f32[6]{0:T(128)} %scale_hbm.1, f32[1,1024]{1,0:T(1,128)} %bitcast.3, f32[1,1024]{1,0:T(1,128)} %bitcast.4, s32[6,343]{1,0:T(8,128)} %cells_hbm.1, s32[1,128]{1,0:T(1,128)} %bitcast.5), custom_call_target="tpu_custom_call" | custom-call | tf_op jit(solution)/shard_map/pallas_call | solution.py:282
  40.1 0.7 %copy.11 = f32[64,1024]{1,0:T(8,128)} copy(f32[64,1024]{1,0:T(8,128)S(1)} %get-tuple-element.4) | data formatting | bytes 524288
  40.8 0.6 %copy.12 = f32[64,128]{1,0:T(8,128)} copy(f32[64,128]{1,0:T(8,128)S(1)} %get-tuple-element.5) | data formatting | bytes 65536
where the time goes:
time: 41.5 us; the launch traced here: 41.4 us
  Pallas kernels  39.4 us (95%)
  local copies, waits for them, and re-layouts  1.32 us (3%)
  between operations  0.64 us (2%)
    pallas_call x1, Pallas kernels, per_device(): pl.pallas_call(functools.partial(kernel, n_band, n_dom, inner), out_shape...  39.4 us
    unnamed x2, local copies, waits for them, and re-layouts  1.32 us

commit v1 on v0

v1 whole, which is shorter than its diff:
```python
import functools

import jax
import jax.numpy as jnp
from jax import lax
from jax.experimental import pallas as pl
from jax.experimental.pallas import tpu as pltpu
from jax.sharding import PartitionSpec as P

DEGREE = 3
CENTER = 1.0
HALF_WIDTH = 4.0
LANES = 128
PLACES = 2
CHUNKS = 2
F32, BF16 = jnp.float32, jnp.bfloat16


def stacked_parts(value):
    high = value.astype(BF16)
    low = (value - high.astype(F32)).astype(BF16)
    return jnp.concatenate([high, low], axis=0)


def folded(value):
    half = value.shape[0] // 2
    return value[:half] + value[half:]


def dot(a, b):
    return jnp.dot(a, b, preferred_element_type=F32)


def dot_nt(a, b):
    return lax.dot_general(a, b, (((1,), (1,)), ((), ())), preferred_element_type=F32)


def narrow(value):
    return value.astype(jnp.int16)


def one_hot(a, b):
    return jnp.where(a == b, jnp.array(1, BF16), jnp.array(0, BF16))


def kernel(
    n_band, n_dom,
    x_hbm, stiff_hbm, scale_hbm, pot_hbm, mass_hbm, cells_hbm, shared_hbm,
    filt_ref, margin_ref,
    x_ref, stiff_ref, scale_ref, pot_ref, mass_ref, cells_ref, shared_ref, load_sem,
    idx, stiff_pad, weight_main, weight_rest, gather, scatter, spread, lead,
    lead_send, lead_recv, ret_send, ret_recv, part_send, part_recv,
    uu, yy, xx, zz, block_send, block_recv, last_cross,
    own_send, own_recv, own_all, cross_send, cross_all, final,
    lead_sem, ret_sem, part_sem, cross_last_sem, block_sem,
    own_pair_sem, own_line_sem, cross_sem, final_sem,
):
    rows, owned = x_ref.shape
    cells, npc = cells_ref.shape
    shared = shared_ref.shape[1]
    width = idx.shape[1]
    main = weight_main.shape[1]
    rest = width - main
    local = owned + shared
    lines = n_dom // PLACES
    band, dom = lax.axis_index("band"), lax.axis_index("dom")
    after, before = lax.rem(dom + 1, n_dom), lax.rem(dom + n_dom - 1, n_dom)
    place, line = lax.rem(dom, PLACES), dom // PLACES
    partner = line * PLACES + 1 - place

    def turned(value, by, size):
        return lax.rem(value + by, size)

    def at(b, d):
        return {"band": b, "dom": d}

    def spot(l, p):
        return turned(line, l, lines) * PLACES + p

    pairs = (
        (shared_hbm, shared_ref), (mass_hbm, mass_ref), (pot_hbm, pot_ref), (x_hbm, x_ref),
        (cells_hbm, cells_ref), (stiff_hbm, stiff_ref), (scale_hbm, scale_ref))
    loads = [pltpu.make_async_copy(src, dst, load_sem.at[k]) for k, (src, dst) in enumerate(pairs)]
    first_loads, later_loads = loads[:4], loads[4:]
    for load in loads:
        load.start()
    barrier = pltpu.get_barrier_semaphore()
    greeted = []
    for k in range(n_band):
        other = turned(band, k, n_band)
        opposite = turned(band, n_band - k, n_band)
        greeted += [at(other, after), at(opposite, before)]
        if k:
            greeted += [at(other, dom)] + [at(other, spot(l, 1 - place)) for l in range(lines)]
        else:
            greeted += [at(band, partner)] + [at(band, spot(l, place)) for l in range(1, lines)]
    for device in greeted:
        pl.semaphore_signal(barrier, inc=1, device_id=device)

    def remote(src, dst, sems, slot, device):
        return pltpu.make_async_remote_copy(
            src_ref=src, dst_ref=dst, send_sem=sems.at[0, slot], recv_sem=sems.at[1, slot],
            device_id=device, device_id_type=pl.DeviceIdType.MESH)

    started = []

    def send(*args):
        copy = remote(*args)
        copy.start()
        started.append(copy)
        return copy

    for load in first_loads:
        load.wait()
    mass, pot = mass_ref[...], pot_ref[...]
    shared_row = shared_ref[...]
    lead[0:rows, :] = x_ref[...]
    lead[rows:rows + 8, :] = jnp.concatenate(
        [mass, pot, jnp.zeros((6, owned), F32)], axis=0)
    wanted = jnp.broadcast_to(shared_row, (rows + 8, shared))
    lane_of, tile_of = wanted & (LANES - 1), wanted >> 7
    picked = None
    for k in range(owned // LANES):
        found = jnp.take_along_axis(lead[:, k * LANES:(k + 1) * LANES], lane_of, axis=1)
        picked = found if picked is None else jnp.where(tile_of == k, found, picked)
    lead_send[...] = picked
    pl.semaphore_wait(barrier, len(greeted))
    lead_copy = send(lead_send, lead_recv, lead_sem, 0, at(band, before))

    for load in later_loads:
        load.wait()
    uu[...] = stacked_parts(mass * x_ref[...])
    idx[...] = jnp.full(idx.shape, -1, jnp.int32)
    idx[0:cells, 0:npc] = cells_ref[...]
    node = narrow(lax.broadcasted_iota(jnp.int32, (LANES, width), 0))
    lane = narrow(lax.broadcasted_iota(jnp.int32, (width, LANES), 1))
    shared_col = jnp.broadcast_to(shared_row, (LANES, shared)).T
    shared_wide = narrow(jnp.concatenate([shared_col] * (width // LANES), axis=1))
    shared_tall = narrow(jnp.broadcast_to(shared_row, (width, shared)))
    for c in range(cells):
        span = slice(c * width, (c + 1) * width)
        slot_row = narrow(jnp.broadcast_to(idx[c:c + 1, :], (LANES, width)))
        for k in range(local // LANES):
            tile = slice(k * LANES, (k + 1) * LANES)
            gather[tile, span] = one_hot(node + jnp.int16(k * LANES), slot_row)
        gather[local:, span] = one_hot(shared_wide, slot_row)
        yy[:, span] = dot(uu[...], gather[0:owned, span])
    for c in range(cells):
        span = slice(c * width, (c + 1) * width)
        slot_col = narrow(jnp.broadcast_to(idx[c:c + 1, :], (LANES, width)).T)
        for k in range(local // LANES):
            tile = slice(k * LANES, (k + 1) * LANES)
            scatter[span, tile] = one_hot(lane + jnp.int16(k * LANES), slot_col)
        scatter[span, local:] = one_hot(shared_tall, slot_col)
    short = narrow(shared_col)
    lane = narrow(lax.broadcasted_iota(jnp.int32, (shared, LANES), 1))
    for k in range(owned // LANES):
        spread[:, k * LANES:(k + 1) * LANES] = one_hot(lane + jnp.int16(k * LANES), short)
    stiff_pad[...] = jnp.zeros(stiff_pad.shape, F32)
    stiff_pad[0:npc, 0:npc] = stiff_ref[...]
    stiff = stiff_pad[...]
    high = stiff.astype(BF16)
    low = (stiff - high.astype(F32)).astype(BF16)
    top, bottom = slice(0, main), slice(main, width)
    weight_main[...] = jnp.concatenate(
        [high[top, top], high[top, top]]
        + ([high[bottom, top], high[bottom, top]] if rest else [])
        + [low[top, top]] + ([low[bottom, top]] if rest else []), axis=0)
    if rest:
        edge = jnp.concatenate([high[top, bottom], low[top, bottom]], axis=1)
        corner = jnp.concatenate([high[bottom, bottom], low[bottom, bottom]], axis=1)
        weight_rest[...] = jnp.concatenate([edge, edge, corner, corner], axis=0)

    mass_shared, pot_shared = lead_send[rows:rows + 1, :], lead_send[rows + 1:rows + 2, :]
    partial = x_ref[...]
    current_shared = lead_send[0:rows, :]
    previous, previous_shared = None, None
    returned = None
    for t in range(DEGREE):
        last = t == DEGREE - 1
        factor = (1.0 if t == 0 else 2.0) / HALF_WIDTH
        if t:
            uu[...] = stacked_parts(mass * partial)
            for c in range(cells):
                span = slice(c * width, (c + 1) * width)
                yy[:, span] = dot(uu[...], gather[0:owned, span])
        if t == 0:
            lead_copy.wait_recv()
            mass_ghost = lead_recv[rows:rows + 1, :]
            ghost = lead_recv[0:rows, :]
            fix = None
            outside = stacked_parts(mass_ghost * ghost)
        else:
            ret_copy.wait_recv()
            part_copy.wait_recv()
            fix = earlier * mass_shared * ret_recv[t - 1]
            ghost = part_recv[t - 1] + earlier * mass_ghost * returned
            current_shared = part + fix
            outside = stacked_parts(
                jnp.concatenate([mass_ghost * ghost, mass_shared * fix], axis=1))
        reach = owned + outside.shape[1]
        for c in range(cells):
            span = slice(c * width, (c + 1) * width)
            y = folded(yy[:, span] + dot(outside, gather[owned:reach, span]))
            y_high = y.astype(BF16)
            y_low = (y - y_high.astype(F32)).astype(BF16)
            xx[c * rows:(c + 1) * rows, :] = jnp.concatenate(
                [y_high[:, top], y_low[:, top]]
                + ([y_high[:, bottom], y_low[:, bottom]] if rest else [])
                + [y_high], axis=1)
        z_main = dot(xx[...], weight_main[...])
        if rest:
            z_rest = dot(xx[:, 0:2 * width], weight_rest[...])
        for c in range(cells):
            state = slice(c * rows, (c + 1) * rows)
            z = z_main[state]
            if rest:
                z = jnp.concatenate([z, z_rest[state, 0:rest] + z_rest[state, rest:]], axis=1)
            zz[:, c * width:(c + 1) * width] = stacked_parts(z * scale_ref[c])
        border = folded(dot(zz[...], scatter[:, owned:]))
        returned = border[:, 0:shared]
        ret_send[t] = returned
        ret_copy = send(ret_send.at[t], ret_recv.at[t], ret_sem, t, at(band, after))
        if not last:
            part = factor * (
                mass_shared * border[:, shared:] + (pot_shared - CENTER) * current_shared)
            if t:
                part = part - previous_shared
            part_send[t] = part
            part_copy = send(part_send.at[t], part_recv.at[t], part_sem, t, at(band, before))
        current = partial
        if t:
            current = current + folded(dot(stacked_parts(fix), spread[...]))
        step = owned // CHUNKS if last else owned
        parts = []
        for j in range(owned // step):
            span = slice(j * step, (j + 1) * step)
            sums = folded(dot(zz[...], scatter[:, span]))
            piece = factor * (mass[:, span] * sums + (pot[:, span] - CENTER) * current[:, span])
            if t:
                piece = piece - previous[:, span]
            parts.append(piece)
            if last:
                block_send[j] = piece
                for k in range(1, n_band):
                    other = turned(band, k, n_band)
                    leads = place == jnp.where(band < other, 0, 1)

                    @pl.when(jnp.logical_not(leads))
                    def _():
                        remote(block_send.at[j], block_recv.at[n_band - k - 1, j], block_sem,
                               (k - 1) * CHUNKS + j, at(other, dom)).start()

                    if j == 0:
                        @pl.when(leads)
                        def _():
                            remote(ret_send.at[t], last_cross.at[n_band - k - 1], cross_last_sem,
                                   k - 1, at(other, after)).start()
        partial = jnp.concatenate(parts, axis=1) if last else parts[0]
        previous, previous_shared = current, current_shared
        earlier = factor

    scaling = 1.0 / (owned * n_dom)

    def packed(block):
        return jnp.concatenate([block[0:rows // 2], block[rows // 2:]], axis=1) * scaling

    def product(mine, theirs):
        both = folded(dot_nt(mine, theirs))
        return packed(both[:, 0:rows] + both[:, rows:])

    def mended(block, returned):
        fix = stacked_parts(earlier * mass_shared * returned)
        return block + folded(dot(fix, spread[...]))

    ret_copy.wait_recv()
    filtered = mended(partial, ret_recv[DEGREE - 1])
    filt_ref[...] = filtered
    uu[...] = stacked_parts(filtered)
    own_send[0] = product(uu[...], uu[...])
    pair_copy = send(own_send.at[0], own_recv, own_pair_sem, 0, at(band, partner))
    span = 2 * lines - 1
    for k in range(1, n_band):
        other = turned(band, k, n_band)
        leads = place == jnp.where(band < other, 0, 1)

        @pl.when(leads)
        def _():
            remote(ret_send.at[0], last_cross.at[k - 1], cross_last_sem, n_band - k - 1,
                   at(other, after)).wait_recv()
            for j in range(CHUNKS):
                remote(block_send.at[j], block_recv.at[k - 1, j], block_sem,
                       (n_band - k - 1) * CHUNKS + j, at(other, dom)).wait_recv()
            theirs = stacked_parts(mended(
                jnp.concatenate([block_recv[k - 1, j] for j in range(CHUNKS)], axis=1),
                last_cross[k - 1]))
            cross_send[k - 1, 0] = product(uu[...], theirs)
            cross_send[k - 1, 1] = product(theirs, uu[...])
            for l in range(lines):
                if l:
                    remote(cross_send.at[k - 1, 0], cross_all.at[k - 1, l], cross_sem,
                           (k - 1) * span + l - 1, at(band, spot(l, place))).start()
                remote(cross_send.at[k - 1, 1], cross_all.at[n_band - k - 1, lines + l],
                       cross_sem, (k - 1) * span + lines - 1 + l,
                       at(other, spot(l, 1 - place))).start()

    pair_copy.wait_recv()
    own_send[1] = own_send[0] + own_recv[...]
    gathers = place == jnp.where(band == 0, 1, 0)

    @pl.when(gathers)
    def _():
        for l in range(1, lines):
            remote(own_send.at[1], own_all.at[l], own_line_sem, l - 1,
                   at(band, spot(l, place))).start()

    for k in range(1, n_band):
        other = turned(band, k, n_band)
        leads = place == jnp.where(band < other, 0, 1)

        @pl.when(leads)
        def _():
            total = cross_send[k - 1, 0]
            waits = []
            for l in range(lines):
                if l:
                    waits.append(remote(
                        cross_send.at[k - 1, 0], cross_all.at[k - 1, l], cross_sem,
                        (k - 1) * span + l - 1, at(band, spot(l, place))))
                waits.append(remote(
                    cross_send.at[k - 1, 1], cross_all.at[k - 1, lines + l], cross_sem,
                    (n_band - k - 1) * span + lines - 1 + l, at(other, spot(l, 1 - place))))
            for copy in waits:
                copy.wait_recv()
            for l in range(1, 2 * lines):
                total = total + cross_all[k - 1, l]
            final[k] = total
            remote(final.at[k], final.at[k], final_sem, k, at(band, partner)).start()

    @pl.when(gathers)
    def _():
        for l in range(1, lines):
            remote(own_send.at[1], own_all.at[l], own_line_sem, l - 1,
                   at(band, spot(l, place))).wait()
        total = own_send[1]
        for l in range(1, lines):
            total = total + own_all[l]
        final[0] = total
        remote(final.at[0], final.at[0], final_sem, 0, at(band, partner)).start()

    for k in range(n_band):
        other = turned(band, k, n_band)
        holds = place == jnp.where(band < other, 0, 1) if k else gathers
        copy = remote(final.at[k], final.at[k], final_sem, k, at(band, partner))

        @pl.when(holds)
        def _():
            copy.wait_send()

        @pl.when(jnp.logical_not(holds))
        def _():
            copy.wait_recv()

    pieces = []
    for b in range(n_band):
        piece = final[0]
        for k in range(1, n_band):
            piece = jnp.where(turned(band, k, n_band) == b, final[k], piece)
        pieces.append(jnp.concatenate([piece[:, 0:rows], piece[:, rows:]], axis=0))
    margin_ref[...] = jnp.concatenate(pieces, axis=1)
    for copy in started:
        copy.wait_send()
    for k in range(1, n_band):
        other = turned(band, k, n_band)
        leads = place == jnp.where(band < other, 0, 1)

        @pl.when(leads)
        def _():
            remote(ret_send.at[0], last_cross.at[k - 1], cross_last_sem, k - 1,
                   at(other, after)).wait_send()
            for l in range(lines):
                if l:
                    remote(cross_send.at[k - 1, 0], cross_all.at[k - 1, l], cross_sem,
                           (k - 1) * span + l - 1, at(band, spot(l, place))).wait_send()
                remote(cross_send.at[k - 1, 1], cross_all.at[k - 1, lines + l], cross_sem,
                       (k - 1) * span + lines - 1 + l,
                       at(other, spot(l, 1 - place))).wait_send()

        @pl.when(jnp.logical_not(leads))
        def _():
            for j in range(CHUNKS):
                remote(block_send.at[j], block_recv.at[k - 1, j], block_sem,
                       (k - 1) * CHUNKS + j, at(other, dom)).wait_send()


def rounded_up(value):
    return -(-value // LANES) * LANES


def per_device(
    n_band, n_dom,
    states_in, stiffness, cell_scale, potential, inv_mass_sqrt, cell_nodes, shared_nodes
):
    rows, owned = states_in.shape
    cells, npc = cell_nodes.shape
    shared = shared_nodes.shape[0]
    width = rounded_up(npc)
    nodes = owned + 2 * shared
    states = n_band * rows
    main = width // (2 * LANES) * 2 * LANES
    rest = width - main
    lines = n_dom // PLACES
    others = n_band - 1
    block = (rows // 2, 2 * rows)
    pairs = lambda count: pltpu.SemaphoreType.DMA((2, count))
    vmem = pltpu.VMEM
    in_vmem = pl.BlockSpec(memory_space=pltpu.VMEM)
    return pl.pallas_call(
        functools.partial(kernel, n_band, n_dom),
        out_shape=(
            jax.ShapeDtypeStruct((rows, owned), F32),
            jax.ShapeDtypeStruct((rows, states), F32),
        ),
        in_specs=[pl.BlockSpec(memory_space=pltpu.HBM)] * 7,
        out_specs=(in_vmem, in_vmem),
        scratch_shapes=[
            vmem((rows, owned), F32),
            vmem((npc, npc), F32),
            pltpu.SMEM((cells,), F32),
            vmem((1, owned), F32),
            vmem((1, owned), F32),
            vmem((cells, npc), jnp.int32),
            vmem((1, shared), jnp.int32),
            pltpu.SemaphoreType.DMA((7,)),
            vmem((-(-cells // 8) * 8, width), jnp.int32),
            vmem((width, width), F32),
            vmem((3 * width, main), BF16),
            vmem((2 * width, 2 * max(rest, LANES)), BF16),
            vmem((nodes, cells * width), BF16),
            vmem((cells * width, nodes), BF16),
            vmem((shared, owned), BF16),
            vmem((rows + 8, owned), F32),
            vmem((rows + 8, shared), F32),
            vmem((rows + 8, shared), F32),
            vmem((DEGREE, rows, shared), F32),
            vmem((DEGREE, rows, shared), F32),
            vmem((DEGREE - 1, rows, shared), F32),
            vmem((DEGREE - 1, rows, shared), F32),
            vmem((2 * rows, owned), BF16),
            vmem((2 * rows, cells * width), F32),
            vmem((cells * rows, 3 * width), BF16),
            vmem((2 * rows, cells * width), BF16),
            vmem((CHUNKS, rows, owned // CHUNKS), F32),
            vmem((others, CHUNKS, rows, owned // CHUNKS), F32),
            vmem((others, rows, shared), F32),
            vmem((2, *block), F32),
            vmem(block, F32),
            vmem((lines, *block), F32),
            vmem((others, 2, *block), F32),
            vmem((others, 2 * lines, *block), F32),
            vmem((n_band, *block), F32),
            pairs(1),
            pairs(DEGREE),
            pairs(DEGREE - 1),
            pairs(others),
            pairs(others * CHUNKS),
            pairs(1),
            pairs(lines - 1),
            pairs(others * (2 * lines - 1)),
            pairs(n_band),
        ],
        compiler_params=pltpu.CompilerParams(collective_id=0, has_side_effects=True, vmem_limit_bytes=28 << 20),
    )(*[pltpu.with_memory_space_constraint(value, pltpu.HBM) for value in (
        states_in, stiffness, cell_scale, potential[None, :], inv_mass_sqrt[None, :],
        cell_nodes, shared_nodes[None, :],
    )])


def solution(mesh):
    n_band, n_dom = mesh.shape["band"], mesh.shape["dom"]
    return jax.shard_map(
        functools.partial(per_device, n_band, n_dom),
        mesh=mesh,
        in_specs=(P("band", "dom"), P(), P("dom"), P("dom"), P("dom"), P("dom", None), P("dom")),
        out_specs=(P("band", "dom"), P("band", None)),
        check_vma=False,
    )
```

time: 41.5 us -> 36 us (0.87)
  Pallas kernels: 39.4 us -> 33.9 us
    pallas_call x1, Pallas kernels: 39.4 us -> 33.9 us  [per_device(): pl.pallas_call(functools.partial(kernel, n_band, n_dom), out_shape=(jax.S...]
where the time goes in v1:
time: 36 us; the launch traced here: 35.9 us
  Pallas kernels  33.9 us (94%)
  local copies, waits for them, and re-layouts  1.32 us (4%)
  between operations  0.64 us (2%)
    pallas_call x1, Pallas kernels, per_device(): pl.pallas_call(functools.partial(kernel, n_band, n_dom), out_shape=(jax.S...  33.9 us
    unnamed x2, local copies, waits for them, and re-layouts  1.32 us

profile of v1, /device:TPU:0, one launch (start us, length us, event | category | flops | bytes accessed | tf_op | source)
XLA Modules:
  0.0 35.9 jit_solution(7396425159200003905)
XLA Ops:
  0.6 33.9 %shard_map.86 = (f32[64,1024]{1,0:T(8,128)S(1)}, f32[64,128]{1,0:T(8,128)S(1)}) custom-call(f32[64,1024]{1,0:T(8,128)} %x_hbm.1, f32[343,343]{1,0:T(8,128)} %stiff_hbm.1, f32[6]{0:T(128)} %scale_hbm.1, f32[1,1024]{1,0:T(1,128)} %bitcast.3, f32[1,1024]{1,0:T(1,128)} %bitcast.4, s32[6,343]{1,0:T(8,128)} %cells_hbm.1, s32[1,128]{1,0:T(1,128)} %bitcast.5), custom_call_target="tpu_custom_call" | custom-call | tf_op jit(solution)/shard_map/pallas_call | solution.py:418
  34.6 0.7 %copy.11 = f32[64,1024]{1,0:T(8,128)} copy(f32[64,1024]{1,0:T(8,128)S(1)} %get-tuple-element.4) | data formatting | bytes 524288
  35.3 0.6 %copy.12 = f32[64,128]{1,0:T(8,128)} copy(f32[64,128]{1,0:T(8,128)S(1)} %get-tuple-element.5) | data formatting | bytes 65536

commit v2 on v1

--- a/solution.py
+++ b/solution.py
@@ -12,7 +12,7 @@
 HALF_WIDTH = 4.0
 LANES = 128
 PLACES = 2
-CHUNKS = 2
+CHUNKS = 4
 F32, BF16 = jnp.float32, jnp.bfloat16
 
 
@@ -53,7 +53,7 @@
     uu, yy, xx, zz, block_send, block_recv, last_cross,
     own_send, own_recv, own_all, cross_send, cross_all, final,
     lead_sem, ret_sem, part_sem, cross_last_sem, block_sem,
-    own_pair_sem, own_line_sem, cross_sem, final_sem,
+    own_pair_sem, own_line_sem, cross_sem, final_sem, known_sem,
 ):
     rows, owned = x_ref.shape
     cells, npc = cells_ref.shape
@@ -82,20 +82,27 @@
         (cells_hbm, cells_ref), (stiff_hbm, stiff_ref), (scale_hbm, scale_ref))
     loads = [pltpu.make_async_copy(src, dst, load_sem.at[k]) for k, (src, dst) in enumerate(pairs)]
     first_loads, later_loads = loads[:4], loads[4:]
+    barrier = pltpu.get_barrier_semaphore()
+    others = [at(turned(band, k, n_band), dom) for k in range(1, n_band)]
+    greeted = [at(band, after), at(band, before)] + others
+    for device in greeted:
+        pl.semaphore_signal(barrier, inc=1, device_id=device)
     for load in loads:
         load.start()
-    barrier = pltpu.get_barrier_semaphore()
-    greeted = []
-    for k in range(n_band):
-        other = turned(band, k, n_band)
-        opposite = turned(band, n_band - k, n_band)
-        greeted += [at(other, after), at(opposite, before)]
-        if k:
-            greeted += [at(other, dom)] + [at(other, spot(l, 1 - place)) for l in range(lines)]
-        else:
-            greeted += [at(band, partner)] + [at(band, spot(l, place)) for l in range(1, lines)]
-    for device in greeted:
-        pl.semaphore_signal(barrier, inc=1, device_id=device)
+
+    rounds = []
+    reach = 1
+    while reach * 4 <= n_dom or not rounds:
+        there = [at(band, lax.rem(dom + reach, n_dom)), at(band, lax.rem(dom + n_dom - reach, n_dom))]
+        rounds.append(there + (others if reach == 1 else []))
+        reach *= 2
+
+    def tell(r):
+        for device in rounds[r]:
+            pl.semaphore_signal(known_sem.at[r], inc=1, device_id=device)
+
+    def learn(r):
+        pl.semaphore_wait(known_sem.at[r], len(rounds[r]))
 
     def remote(src, dst, sems, slot, device):
         return pltpu.make_async_remote_copy(
@@ -126,6 +133,7 @@
     lead_send[...] = picked
     pl.semaphore_wait(barrier, len(greeted))
     lead_copy = send(lead_send, lead_recv, lead_sem, 0, at(band, before))
+    tell(0)
 
     for load in later_loads:
         load.wait()
@@ -186,6 +194,9 @@
                 yy[:, span] = dot(uu[...], gather[0:owned, span])
         if t == 0:
             lead_copy.wait_recv()
+            learn(0)
+            if len(rounds) > 1:
+                tell(1)
             mass_ghost = lead_recv[rows:rows + 1, :]
             ghost = lead_recv[0:rows, :]
             fix = None
@@ -193,15 +204,19 @@
         else:
             ret_copy.wait_recv()
             part_copy.wait_recv()
+            for r in range(t, len(rounds) if t == DEGREE - 1 else t + 1):
+                learn(r)
+                if r + 1 < len(rounds):
+                    tell(r + 1)
             fix = earlier * mass_shared * ret_recv[t - 1]
             ghost = part_recv[t - 1] + earlier * mass_ghost * returned
             current_shared = part + fix
             outside = stacked_parts(
                 jnp.concatenate([mass_ghost * ghost, mass_shared * fix], axis=1))
-        reach = owned + outside.shape[1]
+        stop = owned + outside.shape[1]
         for c in range(cells):
             span = slice(c * width, (c + 1) * width)
-            y = folded(yy[:, span] + dot(outside, gather[owned:reach, span]))
+            y = folded(yy[:, span] + dot(outside, gather[owned:stop, span]))
             y_high = y.astype(BF16)
             y_low = (y - y_high.astype(F32)).astype(BF16)
             xx[c * rows:(c + 1) * rows, :] = jnp.concatenate(
@@ -221,7 +236,15 @@
         returned = border[:, 0:shared]
         ret_send[t] = returned
         ret_copy = send(ret_send.at[t], ret_recv.at[t], ret_sem, t, at(band, after))
-        if not last:
+        if last:
+            for k in range(1, n_band):
+                other = turned(band, k, n_band)
+
+                @pl.when(place == jnp.where(band < other, 0, 1))
+                def _():
+                    remote(ret_send.at[t], last_cross.at[n_band - k - 1], cross_last_sem,
+                           k - 1, at(other, after)).start()
+        else:
             part = factor * (
                 mass_shared * border[:, shared:] + (pot_shared - CENTER) * current_shared)
             if t:
@@ -250,12 +273,6 @@
                     def _():
                         remote(block_send.at[j], block_recv.at[n_band - k - 1, j], block_sem,
                                (k - 1) * CHUNKS + j, at(other, dom)).start()
-
-                    if j == 0:
-                        @pl.when(leads)
-                        def _():
-                            remote(ret_send.at[t], last_cross.at[n_band - k - 1], cross_last_sem,
-                                   k - 1, at(other, after)).start()
         partial = jnp.concatenate(parts, axis=1) if last else parts[0]
         previous, previous_shared = current, current_shared
         earlier = factor
@@ -393,6 +410,16 @@
                        (k - 1) * CHUNKS + j, at(other, dom)).wait_send()
 
 
+def finish(filt_ref, margin_ref, filt_out, margin_out, sem):
+    copies = [
+        pltpu.make_async_copy(filt_ref, filt_out, sem.at[0]),
+        pltpu.make_async_copy(margin_ref, margin_out, sem.at[1])]
+    for copy in copies:
+        copy.start()
+    for copy in copies:
+        copy.wait()
+
+
 def rounded_up(value):
     return -(-value // LANES) * LANES
 
@@ -415,7 +442,7 @@
     pairs = lambda count: pltpu.SemaphoreType.DMA((2, count))
     vmem = pltpu.VMEM
     in_vmem = pl.BlockSpec(memory_space=pltpu.VMEM)
-    return pl.pallas_call(
+    found = pl.pallas_call(
         functools.partial(kernel, n_band, n_dom),
         out_shape=(
             jax.ShapeDtypeStruct((rows, owned), F32),
@@ -468,12 +495,20 @@
             pairs(lines - 1),
             pairs(others * (2 * lines - 1)),
             pairs(n_band),
+            pltpu.SemaphoreType.REGULAR((max(n_dom.bit_length() - 2, 1),)),
         ],
         compiler_params=pltpu.CompilerParams(collective_id=0, has_side_effects=True, vmem_limit_bytes=28 << 20),
     )(*[pltpu.with_memory_space_constraint(value, pltpu.HBM) for value in (
         states_in, stiffness, cell_scale, potential[None, :], inv_mass_sqrt[None, :],
         cell_nodes, shared_nodes[None, :],
     )])
+    return pl.pallas_call(
+        finish,
+        out_shape=tuple(jax.ShapeDtypeStruct(value.shape, F32) for value in found),
+        in_specs=[in_vmem, in_vmem],
+        out_specs=(pl.BlockSpec(memory_space=pltpu.HBM),) * 2,
+        scratch_shapes=[pltpu.SemaphoreType.DMA((2,))],
+    )(*[pltpu.with_memory_space_constraint(value, pltpu.VMEM) for value in found])
 
 
 def solution(mesh):

time: 36 us -> 34 us (0.944)
  local copies, waits for them, and re-layouts: 1.32 us -> 0 us
  Pallas kernels: 33.9 us -> 33.2 us
    pallas_call x1, Pallas kernels: 33.9 us -> 32.5 us  [per_device(): pl.pallas_call(functools.partial(kernel, n_band, n_dom), out_shape=(jax.S...]
    unnamed x2 -> x0, local copies, waits for them, and re-layouts: 1.32 us -> none
    pallas_call x0 -> x1, Pallas kernels: none -> 0.72 us  [per_device(): pl.pallas_call(finish, out_shape=tuple((jax.ShapeDtypeStruct(value.shape,...]
where the time goes in v2:
time: 34 us; the launch traced here: 33.9 us
  Pallas kernels  33.2 us (98%)
  between operations  0.64 us (2%)
    pallas_call x1, Pallas kernels, per_device(): pl.pallas_call(functools.partial(kernel, n_band, n_dom), out_shape=(jax.S...  32.5 us
    pallas_call x1, Pallas kernels, per_device(): pl.pallas_call(finish, out_shape=tuple((jax.ShapeDtypeStruct(value.shape,...  0.72 us

profile of v2, /device:TPU:0, one launch (start us, length us, event | category | flops | bytes accessed | tf_op | source)
XLA Modules:
  0.0 33.9 jit_solution(8795929164924351805)
XLA Ops:
  0.6 32.5 %shard_map.86 = (f32[64,1024]{1,0:T(8,128)S(1)}, f32[64,128]{1,0:T(8,128)S(1)}) custom-call(f32[64,1024]{1,0:T(8,128)} %x_hbm.1, f32[343,343]{1,0:T(8,128)} %stiff_hbm.1, f32[6]{0:T(128)} %scale_hbm.1, f32[1,1024]{1,0:T(1,128)} %bitcast.3, f32[1,1024]{1,0:T(1,128)} %bitcast.4, s32[6,343]{1,0:T(8,128)} %cells_hbm.1, s32[1,128]{1,0:T(1,128)} %bitcast.5), custom_call_target="tpu_custom_call" | custom-call | tf_op jit(solution)/shard_map/pallas_call | solution.py:445
  33.1 0.7 %shard_map.87 = (f32[64,1024]{1,0:T(8,128)}, f32[64,128]{1,0:T(8,128)}) custom-call(f32[64,1024]{1,0:T(8,128)S(1)} %get-tuple-element.4.filt_ref, f32[64,128]{1,0:T(8,128)S(1)} %get-tuple-element.5.margin_ref), custom_call_target="tpu_custom_call" | custom-call | tf_op jit(solution)/shard_map/pallas_call | solution.py:505

commit v3 on v2

--- a/solution.py
+++ b/solution.py
@@ -50,7 +50,7 @@
     x_ref, stiff_ref, scale_ref, pot_ref, mass_ref, cells_ref, shared_ref, load_sem,
     idx, stiff_pad, weight_main, weight_rest, gather, scatter, spread, lead,
     lead_send, lead_recv, ret_send, ret_recv, part_send, part_recv,
-    uu, yy, xx, zz, block_send, block_recv, last_cross,
+    uu, yy, xx, zz, tt, weight_edge, block_send, block_recv, last_cross,
     own_send, own_recv, own_all, cross_send, cross_all, final,
     lead_sem, ret_sem, part_sem, cross_last_sem, block_sem,
     own_pair_sem, own_line_sem, cross_sem, final_sem, known_sem,
@@ -170,14 +170,51 @@
     high = stiff.astype(BF16)
     low = (stiff - high.astype(F32)).astype(BF16)
     top, bottom = slice(0, main), slice(main, width)
-    weight_main[...] = jnp.concatenate(
-        [high[top, top], high[top, top]]
-        + ([high[bottom, top], high[bottom, top]] if rest else [])
-        + [low[top, top]] + ([low[bottom, top]] if rest else []), axis=0)
+    weight_main[...] = jnp.concatenate([high[:, top], high[:, top], low[:, top]], axis=0)
     if rest:
-        edge = jnp.concatenate([high[top, bottom], low[top, bottom]], axis=1)
-        corner = jnp.concatenate([high[bottom, bottom], low[bottom, bottom]], axis=1)
-        weight_rest[...] = jnp.concatenate([edge, edge, corner, corner], axis=0)
+        paired = jnp.concatenate([high[:, bottom], low[:, bottom]], axis=1)
+        weight_rest[...] = jnp.concatenate([paired, paired], axis=0)
+
+    def triple(value):
+        value_high = value.astype(BF16)
+        value_low = (value - value_high.astype(F32)).astype(BF16)
+        return jnp.concatenate([value_high, value_low, value_high], axis=1)
+
+    def wide(z_main, z_rest):
+        if not rest:
+            return z_main
+        return jnp.concatenate([z_main, z_rest[:, 0:rest] + z_rest[:, rest:]], axis=1)
+
+    def cell_products(outside):
+        for c in range(cells):
+            span = slice(c * width, (c + 1) * width)
+            y = yy[:, span]
+            if outside is not None:
+                y = folded(y) + folded(dot(outside, gather[owned:owned + outside.shape[1], span]))
+            else:
+                y = folded(y)
+            xx[c * rows:(c + 1) * rows, :] = triple(y)
+        z_main = dot(xx[...], weight_main[...])
+        z_rest = dot(xx[:, 0:2 * width], weight_rest[...]) if rest else None
+        for c in range(cells):
+            state = slice(c * rows, (c + 1) * rows)
+            z = wide(z_main[state], z_rest[state] if rest else None)
+            zz[:, c * width:(c + 1) * width] = stacked_parts(z * scale_ref[c])
+
+    def border_sums():
+        return folded(dot(zz[...], scatter[:, owned:]))
+
+    for c in range(cells):
+        span = slice(c * width, (c + 1) * width)
+        picks = gather[owned:, span]
+        z = wide(
+            dot(jnp.concatenate([picks, picks], axis=1), weight_main[width:, :]),
+            dot(picks, weight_rest[0:width, :]) if rest else None)
+        tt[:, span] = stacked_parts(z * scale_ref[c])
+    response = folded(dot(tt[...], scatter[:, owned:]))
+    response_high = response.astype(BF16)
+    response_low = (response - response_high.astype(F32)).astype(BF16)
+    weight_edge[...] = jnp.concatenate([response_high, response_high, response_low], axis=0)
 
     mass_shared, pot_shared = lead_send[rows:rows + 1, :], lead_send[rows + 1:rows + 2, :]
     partial = x_ref[...]
@@ -192,6 +229,9 @@
             for c in range(cells):
                 span = slice(c * width, (c + 1) * width)
                 yy[:, span] = dot(uu[...], gather[0:owned, span])
+        if not last:
+            cell_products(None)
+            inside = border_sums()
         if t == 0:
             lead_copy.wait_recv()
             learn(0)
@@ -200,39 +240,26 @@
             mass_ghost = lead_recv[rows:rows + 1, :]
             ghost = lead_recv[0:rows, :]
             fix = None
-            outside = stacked_parts(mass_ghost * ghost)
+            outside = mass_ghost * ghost
         else:
             ret_copy.wait_recv()
             part_copy.wait_recv()
-            for r in range(t, len(rounds) if t == DEGREE - 1 else t + 1):
+            for r in range(t, len(rounds) if last else t + 1):
                 learn(r)
                 if r + 1 < len(rounds):
                     tell(r + 1)
             fix = earlier * mass_shared * ret_recv[t - 1]
             ghost = part_recv[t - 1] + earlier * mass_ghost * returned
             current_shared = part + fix
-            outside = stacked_parts(
-                jnp.concatenate([mass_ghost * ghost, mass_shared * fix], axis=1))
-        stop = owned + outside.shape[1]
-        for c in range(cells):
-            span = slice(c * width, (c + 1) * width)
-            y = folded(yy[:, span] + dot(outside, gather[owned:stop, span]))
-            y_high = y.astype(BF16)
-            y_low = (y - y_high.astype(F32)).astype(BF16)
-            xx[c * rows:(c + 1) * rows, :] = jnp.concatenate(
-                [y_high[:, top], y_low[:, top]]
-                + ([y_high[:, bottom], y_low[:, bottom]] if rest else [])
-                + [y_high], axis=1)
-        z_main = dot(xx[...], weight_main[...])
-        if rest:
-            z_rest = dot(xx[:, 0:2 * width], weight_rest[...])
-        for c in range(cells):
-            state = slice(c * rows, (c + 1) * rows)
-            z = z_main[state]
-            if rest:
-                z = jnp.concatenate([z, z_rest[state, 0:rest] + z_rest[state, rest:]], axis=1)
-            zz[:, c * width:(c + 1) * width] = stacked_parts(z * scale_ref[c])
-        border = folded(dot(zz[...], scatter[:, owned:]))
+            outside = jnp.concatenate([mass_ghost * ghost, mass_shared * fix], axis=1)
+        if last:
+            cell_products(stacked_parts(outside))
+            border = border_sums()
+        else:
+            used = outside.shape[1]
+            edge = jnp.concatenate(
+                [weight_edge[k * 2 * shared:k * 2 * shared + used, :] for k in range(3)], axis=0)
+            border = inside + dot(triple(outside), edge)
         returned = border[:, 0:shared]
         ret_send[t] = returned
         ret_copy = send(ret_send.at[t], ret_recv.at[t], ret_sem, t, at(band, after))
@@ -251,6 +278,8 @@
                 part = part - previous_shared
             part_send[t] = part
             part_copy = send(part_send.at[t], part_recv.at[t], part_sem, t, at(band, before))
+        if not last:
+            cell_products(stacked_parts(outside))
         current = partial
         if t:
             current = current + folded(dot(stacked_parts(fix), spread[...]))
@@ -477,6 +506,8 @@
             vmem((2 * rows, cells * width), F32),
             vmem((cells * rows, 3 * width), BF16),
             vmem((2 * rows, cells * width), BF16),
+            vmem((4 * shared, cells * width), BF16),
+            vmem((6 * shared, 2 * shared), BF16),
             vmem((CHUNKS, rows, owned // CHUNKS), F32),
             vmem((others, CHUNKS, rows, owned // CHUNKS), F32),
             vmem((others, rows, shared), F32),
@@ -497,7 +528,7 @@
             pairs(n_band),
             pltpu.SemaphoreType.REGULAR((max(n_dom.bit_length() - 2, 1),)),
         ],
-        compiler_params=pltpu.CompilerParams(collective_id=0, has_side_effects=True, vmem_limit_bytes=28 << 20),
+        compiler_params=pltpu.CompilerParams(collective_id=0, has_side_effects=True, vmem_limit_bytes=44 << 20),
     )(*[pltpu.with_memory_space_constraint(value, pltpu.HBM) for value in (
         states_in, stiffness, cell_scale, potential[None, :], inv_mass_sqrt[None, :],
         cell_nodes, shared_nodes[None, :],

time: 34 us -> 33.1 us (0.974)
  the two profiles are of different devices: /device:TPU:0 before, /device:TPU:27 now
where the time goes in v3:
time: 33.1 us; the launch traced here: 32.9 us
  Pallas kernels  32.3 us (98%)
  between operations  0.64 us (2%)
    pallas_call x1, Pallas kernels, per_device(): pl.pallas_call(functools.partial(kernel, n_band, n_dom), out_shape=(jax.S...  31.6 us
    pallas_call x1, Pallas kernels, per_device(): pl.pallas_call(finish, out_shape=tuple((jax.ShapeDtypeStruct(value.shape,...  0.72 us

profile of v3, /device:TPU:27, one launch (start us, length us, event | category | flops | bytes accessed | tf_op | source)
XLA Modules:
  0.0 32.9 jit_solution(8384408153580270403)
XLA Ops:
  0.6 31.6 %shard_map.86 = (f32[64,1024]{1,0:T(8,128)S(1)}, f32[64,128]{1,0:T(8,128)S(1)}) custom-call(f32[64,1024]{1,0:T(8,128)} %x_hbm.1, f32[343,343]{1,0:T(8,128)} %stiff_hbm.1, f32[6]{0:T(128)} %scale_hbm.1, f32[1,1024]{1,0:T(1,128)} %bitcast.3, f32[1,1024]{1,0:T(1,128)} %bitcast.4, s32[6,343]{1,0:T(8,128)} %cells_hbm.1, s32[1,128]{1,0:T(1,128)} %bitcast.5), custom_call_target="tpu_custom_call" | custom-call | tf_op jit(solution)/shard_map/pallas_call | solution.py:474
  32.2 0.7 %shard_map.87 = (f32[64,1024]{1,0:T(8,128)}, f32[64,128]{1,0:T(8,128)}) custom-call(f32[64,1024]{1,0:T(8,128)S(1)} %get-tuple-element.4.filt_ref, f32[64,128]{1,0:T(8,128)S(1)} %get-tuple-element.5.margin_ref), custom_call_target="tpu_custom_call" | custom-call | tf_op jit(solution)/shard_map/pallas_call | solution.py:536

commit v4 on v3

--- a/solution.py
+++ b/solution.py
@@ -229,9 +229,8 @@
             for c in range(cells):
                 span = slice(c * width, (c + 1) * width)
                 yy[:, span] = dot(uu[...], gather[0:owned, span])
-        if not last:
-            cell_products(None)
-            inside = border_sums()
+        cell_products(None)
+        inside = border_sums()
         if t == 0:
             lead_copy.wait_recv()
             learn(0)
@@ -252,14 +251,10 @@
             ghost = part_recv[t - 1] + earlier * mass_ghost * returned
             current_shared = part + fix
             outside = jnp.concatenate([mass_ghost * ghost, mass_shared * fix], axis=1)
-        if last:
-            cell_products(stacked_parts(outside))
-            border = border_sums()
-        else:
-            used = outside.shape[1]
-            edge = jnp.concatenate(
-                [weight_edge[k * 2 * shared:k * 2 * shared + used, :] for k in range(3)], axis=0)
-            border = inside + dot(triple(outside), edge)
+        used = outside.shape[1]
+        edge = jnp.concatenate(
+            [weight_edge[k * 2 * shared:k * 2 * shared + used, :] for k in range(3)], axis=0)
+        border = inside + dot(triple(outside), edge)
         returned = border[:, 0:shared]
         ret_send[t] = returned
         ret_copy = send(ret_send.at[t], ret_recv.at[t], ret_sem, t, at(band, after))
@@ -278,8 +273,7 @@
                 part = part - previous_shared
             part_send[t] = part
             part_copy = send(part_send.at[t], part_recv.at[t], part_sem, t, at(band, before))
-        if not last:
-            cell_products(stacked_parts(outside))
+        cell_products(stacked_parts(outside))
         current = partial
         if t:
             current = current + folded(dot(stacked_parts(fix), spread[...]))
@@ -334,21 +328,27 @@
         def _():
             remote(ret_send.at[0], last_cross.at[k - 1], cross_last_sem, n_band - k - 1,
                    at(other, after)).wait_recv()
+            fixes = stacked_parts(earlier * mass_shared * last_cross[k - 1])
+            sums = [0.0, 0.0]
             for j in range(CHUNKS):
                 remote(block_send.at[j], block_recv.at[k - 1, j], block_sem,
                        (n_band - k - 1) * CHUNKS + j, at(other, dom)).wait_recv()
-            theirs = stacked_parts(mended(
-                jnp.concatenate([block_recv[k - 1, j] for j in range(CHUNKS)], axis=1),
-                last_cross[k - 1]))
-            cross_send[k - 1, 0] = product(uu[...], theirs)
-            cross_send[k - 1, 1] = product(theirs, uu[...])
-            for l in range(lines):
+                part = slice(j * step, (j + 1) * step)
+                theirs = stacked_parts(
+                    block_recv[k - 1, j] + folded(dot(fixes, spread[:, part])))
+                mine = uu[:, part]
+                sums[0] = sums[0] + folded(dot_nt(mine, theirs))
+                sums[1] = sums[1] + folded(dot_nt(theirs, mine))
+            for j in range(2):
+                cross_send[k - 1, j] = packed(sums[j][:, 0:rows] + sums[j][:, rows:])
+            for l in [*range(1, lines), 0]:
+                off = jnp.where(2 * line < lines, lines - l, l) if l else 0
                 if l:
-                    remote(cross_send.at[k - 1, 0], cross_all.at[k - 1, l], cross_sem,
-                           (k - 1) * span + l - 1, at(band, spot(l, place))).start()
-                remote(cross_send.at[k - 1, 1], cross_all.at[n_band - k - 1, lines + l],
-                       cross_sem, (k - 1) * span + lines - 1 + l,
-                       at(other, spot(l, 1 - place))).start()
+                    remote(cross_send.at[k - 1, 0], cross_all.at[k - 1, off], cross_sem,
+                           (k - 1) * span + off - 1, at(band, spot(off, place))).start()
+                remote(cross_send.at[k - 1, 1], cross_all.at[n_band - k - 1, lines + off],
+                       cross_sem, (k - 1) * span + lines - 1 + off,
+                       at(other, spot(off, 1 - place))).start()
 
     pair_copy.wait_recv()
     own_send[1] = own_send[0] + own_recv[...]

time: 33.1 us -> 33.2 us (level)
  the two profiles are of different devices: /device:TPU:27 before, /device:TPU:9 now
where the time goes in v4:
time: 33.2 us; the launch traced here: 33.1 us
  Pallas kernels  32.5 us (98%)
  between operations  0.64 us (2%)
    pallas_call x1, Pallas kernels, per_device(): pl.pallas_call(functools.partial(kernel, n_band, n_dom), out_shape=(jax.S...  31.7 us
    pallas_call x1, Pallas kernels, per_device(): pl.pallas_call(finish, out_shape=tuple((jax.ShapeDtypeStruct(value.shape,...  0.72 us

profile of v4, /device:TPU:9, one launch (start us, length us, event | category | flops | bytes accessed | tf_op | source)
XLA Modules:
  0.0 33.1 jit_solution(1329298100398854235)
XLA Ops:
  0.6 31.7 %shard_map.86 = (f32[64,1024]{1,0:T(8,128)S(1)}, f32[64,128]{1,0:T(8,128)S(1)}) custom-call(f32[64,1024]{1,0:T(8,128)} %x_hbm.1, f32[343,343]{1,0:T(8,128)} %stiff_hbm.1, f32[6]{0:T(128)} %scale_hbm.1, f32[1,1024]{1,0:T(1,128)} %bitcast.3, f32[1,1024]{1,0:T(1,128)} %bitcast.4, s32[6,343]{1,0:T(8,128)} %cells_hbm.1, s32[1,128]{1,0:T(1,128)} %bitcast.5), custom_call_target="tpu_custom_call" | custom-call | tf_op jit(solution)/shard_map/pallas_call | solution.py:474
  32.4 0.7 %shard_map.87 = (f32[64,1024]{1,0:T(8,128)}, f32[64,128]{1,0:T(8,128)}) custom-call(f32[64,1024]{1,0:T(8,128)S(1)} %get-tuple-element.4.filt_ref, f32[64,128]{1,0:T(8,128)S(1)} %get-tuple-element.5.margin_ref), custom_call_target="tpu_custom_call" | custom-call | tf_op jit(solution)/shard_map/pallas_call | solution.py:536

commit v5 on v4

--- a/solution.py
+++ b/solution.py
@@ -50,7 +50,7 @@
     x_ref, stiff_ref, scale_ref, pot_ref, mass_ref, cells_ref, shared_ref, load_sem,
     idx, stiff_pad, weight_main, weight_rest, gather, scatter, spread, lead,
     lead_send, lead_recv, ret_send, ret_recv, part_send, part_recv,
-    uu, yy, xx, zz, tt, weight_edge, block_send, block_recv, last_cross,
+    uu, yy, xx, zz, tt, weight_edge, weight_own, block_send, block_recv, last_cross,
     own_send, own_recv, own_all, cross_send, cross_all, final,
     lead_sem, ret_sem, part_sem, cross_last_sem, block_sem,
     own_pair_sem, own_line_sem, cross_sem, final_sem, known_sem,
@@ -211,10 +211,14 @@
             dot(jnp.concatenate([picks, picks], axis=1), weight_main[width:, :]),
             dot(picks, weight_rest[0:width, :]) if rest else None)
         tt[:, span] = stacked_parts(z * scale_ref[c])
-    response = folded(dot(tt[...], scatter[:, owned:]))
-    response_high = response.astype(BF16)
-    response_low = (response - response_high.astype(F32)).astype(BF16)
-    weight_edge[...] = jnp.concatenate([response_high, response_high, response_low], axis=0)
+
+    def response(columns):
+        value = folded(dot(tt[...], scatter[:, columns]))
+        value_high = value.astype(BF16)
+        value_low = (value - value_high.astype(F32)).astype(BF16)
+        return jnp.concatenate([value_high, value_high, value_low], axis=0)
+
+    weight_edge[...] = response(slice(owned, owned + 2 * shared))
 
     mass_shared, pot_shared = lead_send[rows:rows + 1, :], lead_send[rows + 1:rows + 2, :]
     partial = x_ref[...]
@@ -231,6 +235,10 @@
                 yy[:, span] = dot(uu[...], gather[0:owned, span])
         cell_products(None)
         inside = border_sums()
+        step = owned // CHUNKS if last else owned
+        if last:
+            for j in range(CHUNKS):
+                block_send[j] = folded(dot(zz[...], scatter[:, j * step:(j + 1) * step]))
         if t == 0:
             lead_copy.wait_recv()
             learn(0)
@@ -254,7 +262,8 @@
         used = outside.shape[1]
         edge = jnp.concatenate(
             [weight_edge[k * 2 * shared:k * 2 * shared + used, :] for k in range(3)], axis=0)
-        border = inside + dot(triple(outside), edge)
+        arrived = triple(outside)
+        border = inside + dot(arrived, edge)
         returned = border[:, 0:shared]
         ret_send[t] = returned
         ret_copy = send(ret_send.at[t], ret_recv.at[t], ret_sem, t, at(band, after))
@@ -273,15 +282,18 @@
                 part = part - previous_shared
             part_send[t] = part
             part_copy = send(part_send.at[t], part_recv.at[t], part_sem, t, at(band, before))
-        cell_products(stacked_parts(outside))
+        if not last:
+            cell_products(stacked_parts(outside))
         current = partial
         if t:
             current = current + folded(dot(stacked_parts(fix), spread[...]))
-        step = owned // CHUNKS if last else owned
         parts = []
         for j in range(owned // step):
             span = slice(j * step, (j + 1) * step)
-            sums = folded(dot(zz[...], scatter[:, span]))
+            if last:
+                sums = block_send[j] + dot(arrived, weight_own[:, span])
+            else:
+                sums = folded(dot(zz[...], scatter[:, span]))
             piece = factor * (mass[:, span] * sums + (pot[:, span] - CENTER) * current[:, span])
             if t:
                 piece = piece - previous[:, span]
@@ -297,6 +309,10 @@
                         remote(block_send.at[j], block_recv.at[n_band - k - 1, j], block_sem,
                                (k - 1) * CHUNKS + j, at(other, dom)).start()
         partial = jnp.concatenate(parts, axis=1) if last else parts[0]
+        if not last:
+            share = owned // (DEGREE - 1)
+            columns = slice(t * share, (t + 1) * share)
+            weight_own[:, columns] = response(columns)
         previous, previous_shared = current, current_shared
         earlier = factor
 
@@ -508,6 +524,7 @@
             vmem((2 * rows, cells * width), BF16),
             vmem((4 * shared, cells * width), BF16),
             vmem((6 * shared, 2 * shared), BF16),
+            vmem((6 * shared, owned), BF16),
             vmem((CHUNKS, rows, owned // CHUNKS), F32),
             vmem((others, CHUNKS, rows, owned // CHUNKS), F32),
             vmem((others, rows, shared), F32),

time: 33.2 us -> 33.3 us (level)
  the two profiles are of different devices: /device:TPU:9 before, /device:TPU:0 now
where the time goes in v5:
time: 33.3 us; the launch traced here: 33 us
  Pallas kernels  32.3 us (97%)
  between operations  0.64 us (2%)
    pallas_call x1, Pallas kernels, per_device(): pl.pallas_call(functools.partial(kernel, n_band, n_dom), out_shape=(jax.S...  31.6 us
    pallas_call x1, Pallas kernels, per_device(): pl.pallas_call(finish, out_shape=tuple((jax.ShapeDtypeStruct(value.shape,...  0.72 us

profile of v5, /device:TPU:0, one launch (start us, length us, event | category | flops | bytes accessed | tf_op | source)
XLA Modules:
  0.0 33.0 jit_solution(9591088717841442614)
XLA Ops:
  0.6 31.6 %shard_map.86 = (f32[64,1024]{1,0:T(8,128)S(1)}, f32[64,128]{1,0:T(8,128)S(1)}) custom-call(f32[64,1024]{1,0:T(8,128)} %x_hbm.1, f32[343,343]{1,0:T(8,128)} %stiff_hbm.1, f32[6]{0:T(128)} %scale_hbm.1, f32[1,1024]{1,0:T(1,128)} %bitcast.3, f32[1,1024]{1,0:T(1,128)} %bitcast.4, s32[6,343]{1,0:T(8,128)} %cells_hbm.1, s32[1,128]{1,0:T(1,128)} %bitcast.5), custom_call_target="tpu_custom_call" | custom-call | tf_op jit(solution)/shard_map/pallas_call | solution.py:490
  32.3 0.7 %shard_map.87 = (f32[64,1024]{1,0:T(8,128)}, f32[64,128]{1,0:T(8,128)}) custom-call(f32[64,1024]{1,0:T(8,128)S(1)} %get-tuple-element.4.filt_ref, f32[64,128]{1,0:T(8,128)S(1)} %get-tuple-element.5.margin_ref), custom_call_target="tpu_custom_call" | custom-call | tf_op jit(solution)/shard_map/pallas_call | solution.py:553

commit v6 on v4

--- a/solution.py
+++ b/solution.py
@@ -81,7 +81,7 @@
         (shared_hbm, shared_ref), (mass_hbm, mass_ref), (pot_hbm, pot_ref), (x_hbm, x_ref),
         (cells_hbm, cells_ref), (stiff_hbm, stiff_ref), (scale_hbm, scale_ref))
     loads = [pltpu.make_async_copy(src, dst, load_sem.at[k]) for k, (src, dst) in enumerate(pairs)]
-    first_loads, later_loads = loads[:4], loads[4:]
+    first_loads, later_loads = loads[:5], loads[5:]
     barrier = pltpu.get_barrier_semaphore()
     others = [at(turned(band, k, n_band), dom) for k in range(1, n_band)]
     greeted = [at(band, after), at(band, before)] + others
@@ -131,12 +131,6 @@
         found = jnp.take_along_axis(lead[:, k * LANES:(k + 1) * LANES], lane_of, axis=1)
         picked = found if picked is None else jnp.where(tile_of == k, found, picked)
     lead_send[...] = picked
-    pl.semaphore_wait(barrier, len(greeted))
-    lead_copy = send(lead_send, lead_recv, lead_sem, 0, at(band, before))
-    tell(0)
-
-    for load in later_loads:
-        load.wait()
     uu[...] = stacked_parts(mass * x_ref[...])
     idx[...] = jnp.full(idx.shape, -1, jnp.int32)
     idx[0:cells, 0:npc] = cells_ref[...]
@@ -152,9 +146,15 @@
             tile = slice(k * LANES, (k + 1) * LANES)
             gather[tile, span] = one_hot(node + jnp.int16(k * LANES), slot_row)
         gather[local:, span] = one_hot(shared_wide, slot_row)
-        yy[:, span] = dot(uu[...], gather[0:owned, span])
+    pl.semaphore_wait(barrier, len(greeted))
+    lead_copy = send(lead_send, lead_recv, lead_sem, 0, at(band, before))
+    tell(0)
+
+    for load in later_loads:
+        load.wait()
     for c in range(cells):
         span = slice(c * width, (c + 1) * width)
+        yy[:, span] = dot(uu[...], gather[0:owned, span])
         slot_col = narrow(jnp.broadcast_to(idx[c:c + 1, :], (LANES, width)).T)
         for k in range(local // LANES):
             tile = slice(k * LANES, (k + 1) * LANES)

time: 33.2 us -> 33 us (level)
  no operation moved by 1% of the time
where the time goes in v6:
time: 33 us; the launch traced here: 32.8 us
  Pallas kernels  32.2 us (98%)
  between operations  0.64 us (2%)
    pallas_call x1, Pallas kernels, per_device(): pl.pallas_call(functools.partial(kernel, n_band, n_dom), out_shape=(jax.S...  31.5 us
    pallas_call x1, Pallas kernels, per_device(): pl.pallas_call(finish, out_shape=tuple((jax.ShapeDtypeStruct(value.shape,...  0.72 us

profile of v6, /device:TPU:9, one launch (start us, length us, event | category | flops | bytes accessed | tf_op | source)
XLA Modules:
  0.0 32.8 jit_solution(4153813160237603867)
XLA Ops:
  0.6 31.5 %shard_map.86 = (f32[64,1024]{1,0:T(8,128)S(1)}, f32[64,128]{1,0:T(8,128)S(1)}) custom-call(f32[64,1024]{1,0:T(8,128)} %x_hbm.1, f32[343,343]{1,0:T(8,128)} %stiff_hbm.1, f32[6]{0:T(128)} %scale_hbm.1, f32[1,1024]{1,0:T(1,128)} %bitcast.3, f32[1,1024]{1,0:T(1,128)} %bitcast.4, s32[6,343]{1,0:T(8,128)} %cells_hbm.1, s32[1,128]{1,0:T(1,128)} %bitcast.5), custom_call_target="tpu_custom_call" | custom-call | tf_op jit(solution)/shard_map/pallas_call | solution.py:474
  32.1 0.7 %shard_map.87 = (f32[64,1024]{1,0:T(8,128)}, f32[64,128]{1,0:T(8,128)}) custom-call(f32[64,1024]{1,0:T(8,128)S(1)} %get-tuple-element.4.filt_ref, f32[64,128]{1,0:T(8,128)S(1)} %get-tuple-element.5.margin_ref), custom_call_target="tpu_custom_call" | custom-call | tf_op jit(solution)/shard_map/pallas_call | solution.py:536

commit v7 on v6

--- a/solution.py
+++ b/solution.py
@@ -258,15 +258,7 @@
         returned = border[:, 0:shared]
         ret_send[t] = returned
         ret_copy = send(ret_send.at[t], ret_recv.at[t], ret_sem, t, at(band, after))
-        if last:
-            for k in range(1, n_band):
-                other = turned(band, k, n_band)
-
-                @pl.when(place == jnp.where(band < other, 0, 1))
-                def _():
-                    remote(ret_send.at[t], last_cross.at[n_band - k - 1], cross_last_sem,
-                           k - 1, at(other, after)).start()
-        else:
+        if not last:
             part = factor * (
                 mass_shared * border[:, shared:] + (pot_shared - CENTER) * current_shared)
             if t:
@@ -296,6 +288,12 @@
                     def _():
                         remote(block_send.at[j], block_recv.at[n_band - k - 1, j], block_sem,
                                (k - 1) * CHUNKS + j, at(other, dom)).start()
+
+                    if j == 0:
+                        @pl.when(leads)
+                        def _():
+                            remote(ret_send.at[t], last_cross.at[n_band - k - 1],
+                                   cross_last_sem, k - 1, at(other, after)).start()
         partial = jnp.concatenate(parts, axis=1) if last else parts[0]
         previous, previous_shared = current, current_shared
         earlier = factor
@@ -341,9 +339,8 @@
                 sums[1] = sums[1] + folded(dot_nt(theirs, mine))
             for j in range(2):
                 cross_send[k - 1, j] = packed(sums[j][:, 0:rows] + sums[j][:, rows:])
-            for l in [*range(1, lines), 0]:
-                off = jnp.where(2 * line < lines, lines - l, l) if l else 0
-                if l:
+            for off in [*range(1, lines), 0]:
+                if off:
                     remote(cross_send.at[k - 1, 0], cross_all.at[k - 1, off], cross_sem,
                            (k - 1) * span + off - 1, at(band, spot(off, place))).start()
                 remote(cross_send.at[k - 1, 1], cross_all.at[n_band - k - 1, lines + off],

time: 33 us -> 32.3 us (0.979)
  the two profiles are of different devices: /device:TPU:9 before, /device:TPU:27 now
where the time goes in v7:
time: 32.3 us; the launch traced here: 32.1 us
  Pallas kernels  31.5 us (98%)
  between operations  0.64 us (2%)
    pallas_call x1, Pallas kernels, per_device(): pl.pallas_call(functools.partial(kernel, n_band, n_dom), out_shape=(jax.S...  30.8 us
    pallas_call x1, Pallas kernels, per_device(): pl.pallas_call(finish, out_shape=tuple((jax.ShapeDtypeStruct(value.shape,...  0.72 us

profile of v7, /device:TPU:27, one launch (start us, length us, event | category | flops | bytes accessed | tf_op | source)
XLA Modules:
  0.0 32.1 jit_solution(3973371684927132079)
XLA Ops:
  0.6 30.8 %shard_map.86 = (f32[64,1024]{1,0:T(8,128)S(1)}, f32[64,128]{1,0:T(8,128)S(1)}) custom-call(f32[64,1024]{1,0:T(8,128)} %x_hbm.1, f32[343,343]{1,0:T(8,128)} %stiff_hbm.1, f32[6]{0:T(128)} %scale_hbm.1, f32[1,1024]{1,0:T(1,128)} %bitcast.3, f32[1,1024]{1,0:T(1,128)} %bitcast.4, s32[6,343]{1,0:T(8,128)} %cells_hbm.1, s32[1,128]{1,0:T(1,128)} %bitcast.5), custom_call_target="tpu_custom_call" | custom-call | tf_op jit(solution)/shard_map/pallas_call | solution.py:471
  31.4 0.7 %shard_map.87 = (f32[64,1024]{1,0:T(8,128)}, f32[64,128]{1,0:T(8,128)}) custom-call(f32[64,1024]{1,0:T(8,128)S(1)} %get-tuple-element.4.filt_ref, f32[64,128]{1,0:T(8,128)S(1)} %get-tuple-element.5.margin_ref), custom_call_target="tpu_custom_call" | custom-call | tf_op jit(solution)/shard_map/pallas_call | solution.py:533

commit v8 on v7

--- a/solution.py
+++ b/solution.py
@@ -146,6 +146,7 @@
             tile = slice(k * LANES, (k + 1) * LANES)
             gather[tile, span] = one_hot(node + jnp.int16(k * LANES), slot_row)
         gather[local:, span] = one_hot(shared_wide, slot_row)
+        yy[:, span] = dot(uu[...], gather[0:owned, span])
     pl.semaphore_wait(barrier, len(greeted))
     lead_copy = send(lead_send, lead_recv, lead_sem, 0, at(band, before))
     tell(0)
@@ -154,7 +155,6 @@
         load.wait()
     for c in range(cells):
         span = slice(c * width, (c + 1) * width)
-        yy[:, span] = dot(uu[...], gather[0:owned, span])
         slot_col = narrow(jnp.broadcast_to(idx[c:c + 1, :], (LANES, width)).T)
         for k in range(local // LANES):
             tile = slice(k * LANES, (k + 1) * LANES)

time: 32.3 us -> 31.9 us (0.988)
  the two profiles are of different devices: /device:TPU:27 before, /device:TPU:0 now
where the time goes in v8:
time: 31.9 us; the launch traced here: 31.6 us
  Pallas kernels  31 us (97%)
  between operations  0.64 us (2%)
    pallas_call x1, Pallas kernels, per_device(): pl.pallas_call(functools.partial(kernel, n_band, n_dom), out_shape=(jax.S...  30.3 us
    pallas_call x1, Pallas kernels, per_device(): pl.pallas_call(finish, out_shape=tuple((jax.ShapeDtypeStruct(value.shape,...  0.72 us

profile of v8, /device:TPU:0, one launch (start us, length us, event | category | flops | bytes accessed | tf_op | source)
XLA Modules:
  0.0 31.6 jit_solution(5782868135175820936)
XLA Ops:
  0.6 30.3 %shard_map.86 = (f32[64,1024]{1,0:T(8,128)S(1)}, f32[64,128]{1,0:T(8,128)S(1)}) custom-call(f32[64,1024]{1,0:T(8,128)} %x_hbm.1, f32[343,343]{1,0:T(8,128)} %stiff_hbm.1, f32[6]{0:T(128)} %scale_hbm.1, f32[1,1024]{1,0:T(1,128)} %bitcast.3, f32[1,1024]{1,0:T(1,128)} %bitcast.4, s32[6,343]{1,0:T(8,128)} %cells_hbm.1, s32[1,128]{1,0:T(1,128)} %bitcast.5), custom_call_target="tpu_custom_call" | custom-call | tf_op jit(solution)/shard_map/pallas_call | solution.py:471
  30.9 0.7 %shard_map.87 = (f32[64,1024]{1,0:T(8,128)}, f32[64,128]{1,0:T(8,128)}) custom-call(f32[64,1024]{1,0:T(8,128)S(1)} %get-tuple-element.4.filt_ref, f32[64,128]{1,0:T(8,128)S(1)} %get-tuple-element.5.margin_ref), custom_call_target="tpu_custom_call" | custom-call | tf_op jit(solution)/shard_map/pallas_call | solution.py:533

commit v9 on v8

--- a/solution.py
+++ b/solution.py
@@ -282,7 +282,7 @@
                 block_send[j] = piece
                 for k in range(1, n_band):
                     other = turned(band, k, n_band)
-                    leads = place == jnp.where(band < other, 0, 1)
+                    leads = place == jnp.where(band < other, 1, 0)
 
                     @pl.when(jnp.logical_not(leads))
                     def _():
@@ -320,7 +320,7 @@
     span = 2 * lines - 1
     for k in range(1, n_band):
         other = turned(band, k, n_band)
-        leads = place == jnp.where(band < other, 0, 1)
+        leads = place == jnp.where(band < other, 1, 0)
 
         @pl.when(leads)
         def _():
@@ -349,7 +349,7 @@
 
     pair_copy.wait_recv()
     own_send[1] = own_send[0] + own_recv[...]
-    gathers = place == jnp.where(band == 0, 1, 0)
+    gathers = place == jnp.where(band == 0, 0, 1)
 
     @pl.when(gathers)
     def _():
@@ -359,7 +359,7 @@
 
     for k in range(1, n_band):
         other = turned(band, k, n_band)
-        leads = place == jnp.where(band < other, 0, 1)
+        leads = place == jnp.where(band < other, 1, 0)
 
         @pl.when(leads)
         def _():
@@ -393,7 +393,7 @@
 
     for k in range(n_band):
         other = turned(band, k, n_band)
-        holds = place == jnp.where(band < other, 0, 1) if k else gathers
+        holds = place == jnp.where(band < other, 1, 0) if k else gathers
         copy = remote(final.at[k], final.at[k], final_sem, k, at(band, partner))
 
         @pl.when(holds)
@@ -415,7 +415,7 @@
         copy.wait_send()
     for k in range(1, n_band):
         other = turned(band, k, n_band)
-        leads = place == jnp.where(band < other, 0, 1)
+        leads = place == jnp.where(band < other, 1, 0)
 
         @pl.when(leads)
         def _():

time: 31.9 us -> 31 us (0.972)
  Pallas kernels: 31 us -> 30.2 us
    pallas_call x1, Pallas kernels: 30.3 us -> 29.5 us  [per_device(): pl.pallas_call(functools.partial(kernel, n_band, n_dom), out_shape=(jax.S...]
where the time goes in v9:
time: 31 us; the launch traced here: 30.9 us
  Pallas kernels  30.2 us (97%)
  between operations  0.64 us (2%)
    pallas_call x1, Pallas kernels, per_device(): pl.pallas_call(functools.partial(kernel, n_band, n_dom), out_shape=(jax.S...  29.5 us
    pallas_call x1, Pallas kernels, per_device(): pl.pallas_call(finish, out_shape=tuple((jax.ShapeDtypeStruct(value.shape,...  0.72 us

profile of v9, /device:TPU:0, one launch (start us, length us, event | category | flops | bytes accessed | tf_op | source)
XLA Modules:
  0.0 30.9 jit_solution(10325261121063499146)
XLA Ops:
  0.6 29.5 %shard_map.86 = (f32[64,1024]{1,0:T(8,128)S(1)}, f32[64,128]{1,0:T(8,128)S(1)}) custom-call(f32[64,1024]{1,0:T(8,128)} %x_hbm.1, f32[343,343]{1,0:T(8,128)} %stiff_hbm.1, f32[6]{0:T(128)} %scale_hbm.1, f32[1,1024]{1,0:T(1,128)} %bitcast.3, f32[1,1024]{1,0:T(1,128)} %bitcast.4, s32[6,343]{1,0:T(8,128)} %cells_hbm.1, s32[1,128]{1,0:T(1,128)} %bitcast.5), custom_call_target="tpu_custom_call" | custom-call | tf_op jit(solution)/shard_map/pallas_call | solution.py:471
  30.1 0.7 %shard_map.87 = (f32[64,1024]{1,0:T(8,128)}, f32[64,128]{1,0:T(8,128)}) custom-call(f32[64,1024]{1,0:T(8,128)S(1)} %get-tuple-element.4.filt_ref, f32[64,128]{1,0:T(8,128)S(1)} %get-tuple-element.5.margin_ref), custom_call_target="tpu_custom_call" | custom-call | tf_op jit(solution)/shard_map/pallas_call | solution.py:533
